TPU v7x, 32 devices: a whole 2x2x4 slice. The times are simulated.
32 devices in a mesh: tp: 4 (over y, core), dp: 8 (over z, x).
Axes of the slice: x: 2, y: 2, z: 4, core: 2. Of those that a mesh axis runs over, the one named last changes fastest.
Arguments:
- tokens: bfloat16 [24, 1024, 768], P('dp', 'tp'), may hold values from -6 to 6
- lengths: int32 [24], P('dp'), may hold values from 196 to 1024, as said below
- ln_gain: float32 [768], replicated, may hold values from 0.1 to 1.9
- w_qkv: bfloat16 [768, 2304], P(None, 'tp'), may hold values from -0.21875 to 0.21875
- q_gain: float32 [12, 64], P('tp'), may hold values from 0.1 to 1.9
- k_gain: float32 [12, 64], P('tp'), may hold values from 0.1 to 1.9
- w_proj: bfloat16 [768, 768], P('tp'), may hold values from -1.75 to 1.75
- w_fc1: bfloat16 [768, 3072], P(None, 'tp'), may hold values from -0.21875 to 0.21875
- b_fc1: float32 [3072], P('tp'), may hold values from -3 to 3
- w_fc2: bfloat16 [3072, 768], P('tp'), may hold values from -0.109375 to 0.109375
- b_fc2: float32 [768], replicated, may hold values from -2 to 2
- d_out: bfloat16 [24, 1024, 768], P('dp', 'tp'), may hold values from -6 to 6
Outputs:
- output: bfloat16 [24, 1024, 768], P('dp', 'tp')
- d_tokens: float32 [24, 1024, 768], P('dp', 'tp')
- d_ln_gain: float32 [768], replicated
- d_qkv: float32 [768, 2304], P(None, 'tp')
- d_q_gain: float32 [12, 64], P('tp')
- d_k_gain: float32 [12, 64], P('tp')
- d_proj: float32 [768, 768], P('tp')
- d_fc1: float32 [768, 3072], P(None, 'tp')
- d_bias_one: float32 [3072], P('tp')
- d_fc2: float32 [3072, 768], P('tp')
- d_bias_two: float32 [768], replicated
Inputs may be any that keep to these rules, and one draw needn't show every extreme that they name: `lengths`: each image's length is one of 196, 576 and 1024; every draw holds all three.
All inputs are finite; a program needn't handle non-finite values.
Results may differ from a plain program's by a relative error of at most 0.014.
Values may be sent and summed in bfloat16 or wider, within the bound.
No kernel may reach another device: no remote copies, remote signals or barrier semaphores. Data moves between devices by JAX's collectives and lax.ppermute only.
A program may use at most 192 MiB of HBM per device.

v0:
```python
import jax
import jax.numpy as jnp
from jax import lax
from jax.sharding import PartitionSpec as P

epsilon = 1e-06
masked_value = -1e30


def layer_norm(values, scale_gain):
    average = jnp.mean(values, axis=-1, keepdims=True)
    centred = values - average
    variance = jnp.mean(centred * centred, axis=-1, keepdims=True)
    return centred * lax.rsqrt(variance + epsilon) * scale_gain


def gelu_exact(values):
    return jax.nn.gelu(values, approximate=False)


def score_block(queries, keys_normed, length, factor):
    scores = (
        jnp.einsum("qhd,khd->hqk", queries, keys_normed, preferred_element_type=jnp.float32)
        * factor
    )
    visible = lax.broadcasted_iota(jnp.int32, scores.shape, 2) < length
    return (scores, visible)


def forward_keys(factor, operands):
    queries, keys_normed, value_rows, length = operands
    scores, visible = score_block(queries, keys_normed, length, factor)
    masked = jnp.where(visible, scores, masked_value)
    row_peak = jnp.max(masked, axis=-1, keepdims=True)
    exponent = jnp.exp(masked - row_peak)
    row_total = jnp.sum(exponent, axis=-1, keepdims=True)
    probability = (exponent / row_total).astype(jnp.bfloat16)
    attended = jnp.einsum(
        "hqk,khd->qhd", probability, value_rows, preferred_element_type=jnp.float32
    )
    return (attended, row_peak[..., 0] + jnp.log(row_total[..., 0]))


def backward_keys(factor, operands):
    queries, keys_normed, value_rows, d_attended, logsum, length = operands
    scores, visible = score_block(queries, keys_normed, length, factor)
    probability = jnp.where(visible, jnp.exp(scores - logsum[..., None]), 0.0)
    d_probs = jnp.einsum("qhd,khd->hqk", d_attended, value_rows, preferred_element_type=jnp.float32)
    row_dot = jnp.sum(probability * d_probs, axis=-1, keepdims=True)
    d_scores = (probability * (d_probs - row_dot)).astype(jnp.bfloat16)
    d_queries = (
        jnp.einsum("hqk,khd->qhd", d_scores, keys_normed, preferred_element_type=jnp.float32)
        * factor
    )
    d_keys = (
        jnp.einsum("hqk,qhd->khd", d_scores, queries, preferred_element_type=jnp.float32) * factor
    )
    d_values = jnp.einsum(
        "hqk,qhd->khd",
        probability.astype(jnp.bfloat16),
        d_attended,
        preferred_element_type=jnp.float32,
    )
    return (d_queries, d_keys, d_values)


def shards(
    tokens, lengths, ln_gain, w_qkv, q_gain, k_gain, w_proj, w_fc1, b_fc1, w_fc2, b_fc2, d_out
):
    images = tokens.shape[0]
    heads_here = q_gain.shape[0]
    head_size = q_gain.shape[1]
    factor = head_size ** (-0.5)
    tokens_float = tokens.astype(jnp.float32)
    normed_local = layer_norm(tokens_float, ln_gain).astype(jnp.bfloat16)
    normed = lax.all_gather(normed_local, "tp", axis=1, tiled=True)
    seq_len = normed.shape[1]
    joined = jnp.einsum("bsd,dc->bsc", normed, w_qkv, preferred_element_type=jnp.float32)
    split_heads = joined.reshape(images, seq_len, heads_here, 3, head_size)
    query_raw = split_heads[:, :, :, 0]
    key_raw = split_heads[:, :, :, 1]
    queries = layer_norm(query_raw, q_gain).astype(jnp.bfloat16)
    keys_normed = layer_norm(key_raw, k_gain).astype(jnp.bfloat16)
    value_rows = split_heads[:, :, :, 2].astype(jnp.bfloat16)

    def attend_image(operands):
        return forward_keys(factor, operands)

    attended, logsum = lax.map(attend_image, (queries, keys_normed, value_rows, lengths))
    attended = attended.reshape(images, seq_len, heads_here * head_size).astype(jnp.bfloat16)
    hidden = jnp.einsum("bsd,df->bsf", normed, w_fc1, preferred_element_type=jnp.float32) + b_fc1
    active = gelu_exact(hidden).astype(jnp.bfloat16)
    partial_sum = jnp.einsum("bsc,cd->bsd", attended, w_proj, preferred_element_type=jnp.float32)
    partial_sum = partial_sum + jnp.einsum(
        "bsf,fd->bsd", active, w_fc2, preferred_element_type=jnp.float32
    )
    summed = lax.psum_scatter(
        partial_sum.astype(jnp.bfloat16), "tp", scatter_dimension=1, tiled=True
    ).astype(jnp.float32)
    output = (tokens_float + summed + b_fc2).astype(jnp.bfloat16)
    d_rows = lax.all_gather(d_out, "tp", axis=1, tiled=True)
    d_fc2 = jnp.einsum("bsf,bsd->fd", active, d_rows, preferred_element_type=jnp.float32)
    d_proj = jnp.einsum("bsc,bsd->cd", attended, d_rows, preferred_element_type=jnp.float32)
    d_active = jnp.einsum("bsd,fd->bsf", d_rows, w_fc2, preferred_element_type=jnp.float32)
    _, gelu_back = jax.vjp(gelu_exact, hidden)
    d_hidden = gelu_back(d_active)[0].astype(jnp.bfloat16)
    d_fc1 = jnp.einsum("bsd,bsf->df", normed, d_hidden, preferred_element_type=jnp.float32)
    d_bias_one = jnp.sum(d_hidden, axis=(0, 1), dtype=jnp.float32)
    d_normed = jnp.einsum("bsf,df->bsd", d_hidden, w_fc1, preferred_element_type=jnp.float32)
    d_attended = jnp.einsum(
        "bsd,cd->bsc", d_rows, w_proj, preferred_element_type=jnp.float32
    ).astype(jnp.bfloat16)
    d_heads = d_attended.reshape(images, seq_len, heads_here, head_size)

    def back_image(operands):
        return backward_keys(factor, operands)

    d_queries, d_keys, d_values = lax.map(
        back_image, (queries, keys_normed, value_rows, d_heads, logsum, lengths)
    )
    _, query_back = jax.vjp(layer_norm, query_raw, q_gain)
    d_query_raw, d_q_gain = query_back(d_queries)
    _, key_back = jax.vjp(layer_norm, key_raw, k_gain)
    d_key_raw, d_k_gain = key_back(d_keys)
    d_joined = (
        jnp.stack([d_query_raw, d_key_raw, d_values], axis=3)
        .reshape(images, seq_len, -1)
        .astype(jnp.bfloat16)
    )
    d_qkv = jnp.einsum("bsd,bsc->dc", normed, d_joined, preferred_element_type=jnp.float32)
    d_normed = d_normed + jnp.einsum(
        "bsc,dc->bsd", d_joined, w_qkv, preferred_element_type=jnp.float32
    )
    d_local = lax.psum_scatter(
        d_normed.astype(jnp.bfloat16), "tp", scatter_dimension=1, tiled=True
    ).astype(jnp.float32)
    _, norm_back = jax.vjp(layer_norm, tokens_float, ln_gain)
    d_tokens_part, d_ln_gain = norm_back(d_local)
    d_tokens = d_out.astype(jnp.float32) + d_tokens_part
    d_bias_two = jnp.sum(d_out, axis=(0, 1), dtype=jnp.float32)
    d_ln_gain, d_bias_two = lax.psum((d_ln_gain, d_bias_two), ("tp", "dp"))
    d_qkv, d_q_gain, d_k_gain, d_proj, d_fc1, d_bias_one, d_fc2 = (
        lax.psum(d_qkv.astype(jnp.bfloat16), "dp").astype(jnp.float32),
        lax.psum(d_q_gain.astype(jnp.bfloat16), "dp").astype(jnp.float32),
        lax.psum(d_k_gain.astype(jnp.bfloat16), "dp").astype(jnp.float32),
        lax.psum(d_proj.astype(jnp.bfloat16), "dp").astype(jnp.float32),
        lax.psum(d_fc1.astype(jnp.bfloat16), "dp").astype(jnp.float32),
        lax.psum(d_bias_one.astype(jnp.bfloat16), "dp").astype(jnp.float32),
        lax.psum(d_fc2.astype(jnp.bfloat16), "dp").astype(jnp.float32),
    )
    return (
        output,
        d_tokens,
        d_ln_gain,
        d_qkv,
        d_q_gain,
        d_k_gain,
        d_proj,
        d_fc1,
        d_bias_one,
        d_fc2,
        d_bias_two,
    )


def solution(mesh):
    placed = (
        P("dp", "tp", None),
        P("dp"),
        P(),
        P(None, "tp"),
        P("tp", None),
        P("tp", None),
        P("tp", None),
        P(None, "tp"),
        P("tp"),
        P("tp", None),
        P(),
        P("dp", "tp", None),
    )
    return jax.shard_map(
        shards,
        mesh=mesh,
        in_specs=placed,
        out_specs=(
            P("dp", "tp", None),
            P("dp", "tp", None),
            P(),
            P(None, "tp"),
            P("tp", None),
            P("tp", None),
            P("tp", None),
            P(None, "tp"),
            P("tp"),
            P("tp", None),
            P(),
        ),
        check_vma=False,
    )
```

profile of v0, /device:TPU:0, one launch (start us, length us, event | category | flops | bytes accessed | tf_op | source)
XLA Modules:
  0.0 569.2 jit_solution(9019446906122960374)
XLA Ops:
  17.7 36.0 %all-gather.3.cloned.1.call-done = bf16[3,1024,768]{2,1,0:T(8,128)(2,1)} async-done(((bf16[3,256,768]{2,1,0:T(8,128)(2,1)}), bf16[3,1024,768]{2,1,0:T(8,128)(2,1)}) %all-gather.3.cloned.1.call-update) | async-done | bytes 4718608 | tf_op jit(solution)/shard_map/all_gather | solution.py:76
  53.6 4.8 fusion.86
  64.5 37.1 %while.28 = (s32[]{:T(128)}, bf16[3,1024,3,64]{1,3,2,0:T(8,128)(2,1)}, f32[3,3,1024]{2,1,0:T(4,128)}, bf16[3,1024,3,64]{1,3,2,0:T(8,128)(2,1)}, s32[3]{0:T(128)S...) while((s32[]{:T(128)}, bf16[3,1024,3,64]{1,3,2,0:T(8,128)(2,1)}, ...), condition=%wide.region_9.10_spmd.clone, body=%wide.region_6.9_spmd.sunk.clone | while | flops 843053056 | bytes 39823964 | solution.py:89
  68.2 3.2 fusion.152
  72.0 4.9 fusion.153
  80.5 3.2 fusion.152
  84.3 4.9 fusion.153
  92.9 3.2 fusion.152
  96.7 4.9 fusion.153
  101.6 6.0 %convolution_convert_fusion = bf16[3,1024,192]{1,2,0:T(8,128)(2,1)} fusion(bf16[3,1024,768]{2,1,0:T(8,128)(2,1)} %all-gather.5.cloned.1.call-done, bf16[192,768]{1,0:T(8,128)(2,1)} %param.22), kind=kOutput, calls=%fused_computation.126 | convolution fusion | flops 906559488 | bytes 6193152 | tf_op jit(solution)/shard_map/bsd,cd->bsc/dot_general | solution.py:110
  107.6 87.6 %while.29 = (s32[]{:T(128)}, f32[3,1024,3,64]{1,3,2,0:T(8,128)}, f32[3,1024,3,64]{1,3,2,0:T(8,128)}, bf16[3,1024,3,64]{1,3,2,0:T(8,128)(2,1)}, bf16[3,1024,3,64]...) while((s32[]{:T(128)}, f32[3,1024,3,64]{1,3,2,0:T(8,128)}, ...), condition=%wide.region_13.14_spmd.clone, body=%wide.region_11.13_spmd.sunk.clone | while | flops 2060843008 | bytes 124744848 | solution.py:118
  107.8 3.1 fusion.162
  112.9 4.8 multiply_reduce_fusion.9
  117.7 5.6 multiply_convert_fusion.6
  123.3 6.0 %fusion.164 = f32[3,1024,3,64]{1,3,2,0:T(8,128)} fusion(f32[3,1024,3,64]{1,3,2,0:T(8,128)} %get-tuple-element.364, s32[]{:T(128)} %get-tuple-element.362, bf16[3,1024,1024]{1,2,0:T(8,128)(2,1)} %multiply_convert_fusion.6, bf16[3,1024,3,64]{1,3,2,0:T(8,128)(2,1)} %get-tuple-element.378), kind=kOutput, calls=%fused_computation.31.clone.1.clone | convolution fusion | flops 402849792 | bytes 7472128 | tf_op jit(solution)/shard_map/while/body/eval_jaxpr/hqk,qhd->khd/dot_general | solution.py:56
  129.3 3.1 fusion.163
  132.4 4.6 fusion.165
  137.0 2.9 fusion.162
  142.0 4.8 multiply_reduce_fusion.9
  146.8 5.6 multiply_convert_fusion.6
  152.4 6.0 %fusion.164 = f32[3,1024,3,64]{1,3,2,0:T(8,128)} fusion(f32[3,1024,3,64]{1,3,2,0:T(8,128)} %get-tuple-element.364, s32[]{:T(128)} %get-tuple-element.362, bf16[3,1024,1024]{1,2,0:T(8,128)(2,1)} %multiply_convert_fusion.6, bf16[3,1024,3,64]{1,3,2,0:T(8,128)(2,1)} %get-tuple-element.378), kind=kOutput, calls=%fused_computation.31.clone.1.clone | convolution fusion | flops 402849792 | bytes 7472128 | tf_op jit(solution)/shard_map/while/body/eval_jaxpr/hqk,qhd->khd/dot_general | solution.py:56
  158.4 3.1 fusion.163
  161.5 4.6 fusion.165
  166.1 2.9 fusion.162
  171.0 4.8 multiply_reduce_fusion.9
  175.8 5.6 multiply_convert_fusion.6
  181.5 6.0 %fusion.164 = f32[3,1024,3,64]{1,3,2,0:T(8,128)} fusion(f32[3,1024,3,64]{1,3,2,0:T(8,128)} %get-tuple-element.364, s32[]{:T(128)} %get-tuple-element.362, bf16[3,1024,1024]{1,2,0:T(8,128)(2,1)} %multiply_convert_fusion.6, bf16[3,1024,3,64]{1,3,2,0:T(8,128)(2,1)} %get-tuple-element.378), kind=kOutput, calls=%fused_computation.31.clone.1.clone | convolution fusion | flops 402849792 | bytes 7472128 | tf_op jit(solution)/shard_map/while/body/eval_jaxpr/hqk,qhd->khd/dot_general | solution.py:56
  187.5 3.1 fusion.163
  190.6 4.6 fusion.165
  200.0 2.8 multiply_reduce_fusion.1
  207.1 6.4 %fusion.72 = (u8[1024,768]{1,0:T(8,128)(4,1)S(1)}, u8[1024,768]{1,0:T(8,128)(4,1)S(1)}, f32[3,1024,768]{2,1,0:T(8,128)S(1)}) fusion(f32[768]{0:T(1024)S(1)} %copy-done.43, bf16[3,1024,768]{2,1,0:T(8,128)(2,1)S(1)} %bitcast.228, bf16[768,768]{1,0:T(8,128)(2,1)S(1)} %copy-done), kind=kOutput, calls=%fused_computation.122 | convolution fusion | flops 3655335936 | bytes 16911360 | tf_op jit(solution)/shard_map/bsd,df->bsf/dot_general | solution.py:91
  213.5 23.0 %multiply_convert_fusion.1 = (bf16[3,1024,768]{2,1,0:T(8,128)(2,1)S(1)}, f32[3,1024,768]{2,1,0:T(8,128)}) fusion(f32[3,1024,768]{2,1,0:T(8,128)S(1)} %get-tuple-element.172, f32[768]{0:T(1024)S(1)} %copy-done.43, u8[1024,768]{1,0:T(8,128)(4,1)S(1)} %get-tuple-element.109, u8[1024,768]{1,0:T(8,128)(4,1)S(1)} %get-tuple-element.108), kind=kLoop, calls=%fused_computation.70 | loop fusion | flops 167510016 | bytes 25168896 | tf_op jit(solution)/shard_map/convert_element_type | solution.py:92
  236.5 7.9 %bitcast_convert_fusion.2 = bf16[768,576]{0,1:T(8,128)(2,1)} fusion(bf16[3,1024,576]{1,2,0:T(8,128)(2,1)S(1)} %bitcast.224, bf16[3,1024,768]{2,1,0:T(8,128)(2,1)} %all-gather.3.cloned.1.call-done), kind=kOutput, calls=%fused_computation.125 | convolution fusion | flops 2718351360 | bytes 9142272 | tf_op jit(solution)/shard_map/bsd,bsc->dc/dot_general | solution.py:130
  244.4 4.6 fusion.74
  249.0 14.2 %fusion.98 = (bf16[768]{0:T(1024)(128)(2,1)S(1)}, bf16[3,1024,768]{2,1,0:T(8,128)(2,1)}) fusion(f32[3,1024,768]{2,1,0:T(8,128)} %get-tuple-element.160, bf16[3,1024,768]{2,1,0:T(8,128)(2,1)} %all-gather.5.cloned.1.call-done, bf16[768,768]{1,0:T(8,128)(2,1)S(1)} %copy-done.44, f32[3,1024,768]{2,1,0:T(8,128)S(1)} %get-tuple-element.172, f32[768]{0:T(1024)S(1)} %copy-done.43), kind=kOutput, calls=%fused_computation.165 | convolution fusion | flops 3661626624 | bytes 29495808 | tf_op jit(solution)/shard_map/bsd,fd->bsf/dot_general | solution.py:104
  263.2 8.7 %bitcast_convert_fusion.1 = bf16[768,768]{1,0:T(8,128)(2,1)} fusion(bf16[3,1024,768]{2,1,0:T(8,128)(2,1)} %all-gather.3.cloned.1.call-done, bf16[3,1024,768]{2,1,0:T(8,128)(2,1)} %get-tuple-element.174), kind=kOutput, calls=%fused_computation.108 | convolution fusion | flops 3624468480 | bytes 10616832 | tf_op jit(solution)/shard_map/bsd,bsf->df/dot_general | solution.py:107
  271.9 7.3 %bitcast_convert_fusion = bf16[768,768]{1,0:T(8,128)(2,1)} fusion(bf16[3,1024,768]{2,1,0:T(8,128)(2,1)S(1)} %get-tuple-element.159, bf16[3,1024,768]{2,1,0:T(8,128)(2,1)} %all-gather.5.cloned.1.call-done), kind=kOutput, calls=%fused_computation.107 | convolution fusion | flops 3624468480 | bytes 10616832 | tf_op jit(solution)/shard_map/bsf,bsd->fd/dot_general | solution.py:102
  279.3 5.9 %fusion.81 = f32[3,1024,768]{2,1,0:T(8,128)S(1)} fusion(bf16[3,1024,768]{2,1,0:T(8,128)(2,1)} %get-tuple-element.174, bf16[768,768]{1,0:T(8,128)(2,1)S(1)} %copy-done), kind=kOutput, calls=%fused_computation.136 | convolution fusion | flops 3623878656 | bytes 15335424 | tf_op jit(solution)/shard_map/bsf,df->bsd/dot_general | solution.py:109
  285.3 5.6 add_convert_fusion
  291.0 6.1 %fusion.79 = f32[3,1024,768]{2,1,0:T(8,128)S(1)} fusion(bf16[3,1024,768]{2,1,0:T(8,128)(2,1)} %copy-done.13, bf16[768,768]{1,0:T(8,128)(2,1)S(1)} %copy-done.44), kind=kOutput, calls=%fused_computation.134 | convolution fusion | flops 3623878656 | bytes 15335424 | tf_op jit(solution)/shard_map/bsf,fd->bsd/dot_general | solution.py:94
  297.1 4.9 add_convert_fusion.2
  302.0 22.5 %all-reduce.1 = (bf16[3,64]{1,0:T(4,128)(2,1)S(1)}, bf16[3,64]{1,0:T(4,128)(2,1)S(1)}, bf16[768]{0:T(1024)(128)(2,1)S(1)}) all-reduce(bf16[3,64]{1,0:T(4,128)(2,1)S(1)} %get-tuple-element.176, bf16[3,64]{1,0:T(4,128)(2,1)S(1)} %get-tuple-element.110, bf16[768]{0:T(1024)(128)(2,1)S(1)} %get-tuple-element.173), channel_id=1, replica_groups=mesh['tp'=4,'dp'=8] {'dp'}, use_global_device_ids=true, to_apply=%region_25.26 | all-reduce | flops 1152 | bytes 4608 | tf_op jit(solution)/shard_map/psum | solution.py:144
  326.3 92.2 %all-reduce.5.cloned.1.call-done = (bf16[768,576]{0,1:T(8,128)(2,1)}, bf16[192,768]{1,0:T(8,128)(2,1)}, bf16[768,768]{1,0:T(8,128)(2,1)}, bf16[768,768]{1,0:T(8,128)(2,1)}) async-done(((bf16[768,576]{0,1:T(8,128)(2,1)}, bf16[192,768]{1,0:T(8,128)(2,1)}, bf16[768,768]{1,0:T(8,128)(2,1)}, bf16[768,768]{1,0:T(8,128)(2,1)}), (bf16[768,576]{0,1:T(8,128)(2,1)}, bf16[192,768]{1,0:T(8,128)(2,1)}, ...) | async-done | bytes 3538960 | tf_op jit(solution)/shard_map/psum | solution.py:143
  418.5 2.9 convert_element_type.130
  425.3 42.6 %reduce-scatter.5.cloned.1.call-done = bf16[3,256,768]{2,1,0:T(8,128)(2,1)} async-done(((bf16[3,1024,768]{2,1,0:T(8,128)(2,1)}), bf16[3,256,768]{2,1,0:T(8,128)(2,1)}) %reduce-scatter.5.cloned.1.call-update) | async-done | bytes 1179664 | tf_op jit(solution)/shard_map/reduce_scatter | solution.py:134
  473.1 45.0 %reduce-scatter.3.cloned.1.call-done = bf16[3,256,768]{2,1,0:T(8,128)(2,1)} async-done(((bf16[3,1024,768]{2,1,0:T(8,128)(2,1)}), bf16[3,256,768]{2,1,0:T(8,128)(2,1)}) %reduce-scatter.3.cloned.1.call-update) | async-done | bytes 1179664 | tf_op jit(solution)/shard_map/reduce_scatter | solution.py:97
  518.1 4.5 convert_reduce_fusion.1
  522.6 39.6 %all-reduce = (f32[768]{0:T(1024)}, f32[768]{0:T(1024)}) all-reduce(f32[768]{0:T(1024)} %get-tuple-element.114, f32[768]{0:T(1024)} %get-tuple-element.169), channel_id=1, replica_groups=mesh['tp'=4,'dp'=8] {'tp','dp'}, use_global_device_ids=true, to_apply=%region_22.23 | all-reduce | flops 1536 | bytes 12288 | tf_op jit(solution)/shard_map/psum | solution.py:141
  (179 shorter events, 54.7 us)
Async XLA Ops:
  7.2 199.6 %copy-start = (bf16[768,768]{1,0:T(8,128)(2,1)S(1)}, bf16[768,768]{1,0:T(8,128)(2,1)}, u32[]{:S(2)}) copy-start(bf16[768,768]{1,0:T(8,128)(2,1)} %param.23) | copy-start | bytes 3538948
  7.2 4.7 copy-start.6
  7.2 4.7 copy-start.34
  7.2 46.4 %all-gather.3.cloned.1.call-start = ((), (), s32[]{:S(2)}) async-start(), calls=%async_computation.2 | async-start | bytes 5898240 | tf_op jit(solution)/shard_map/all_gather | solution.py:76
  8.9 2.4 copy-start.32
  13.3 40.3 %copy-start.45 = (bf16[768,576]{0,1:T(8,128)(2,1)S(1)}, bf16[768,576]{0,1:T(8,128)(2,1)}, u32[]{:S(2)}) copy-start(bf16[768,576]{0,1:T(8,128)(2,1)} %param.19) | copy-start | bytes 2654212
  13.3 88.3 %all-gather.5.cloned.1.call-start = ((), (), s32[]{:S(2)}) async-start(), calls=%async_computation.4 | async-start | bytes 5898240 | tf_op jit(solution)/shard_map/all_gather | solution.py:101
  14.1 404.4 %all-reduce.5.cloned.1.call-start = ((), (), s32[]{:S(2)}) async-start(), calls=%async_computation.6 | async-start | bytes 7077888 | tf_op jit(solution)/shard_map/psum | solution.py:143
  59.2 4.0 copy-start.2
  59.2 4.5 copy-start.4
  60.9 2.3 copy-start.16
  61.3 1.9 copy-start.22
  61.9 1.4 copy-start.41
  62.2 1.5 copy-start.18
  101.6 6.0 %copy-start.8 = (bf16[3,1024,3,64]{1,3,2,0:T(8,128)(2,1)}, bf16[3,1024,3,64]{1,3,2,0:T(8,128)(2,1)S(1)}, u32[]{:S(2)}) copy-start(bf16[3,1024,3,64]{1,3,2,0:T(8,128)(2,1)S(1)} %get-tuple-element.394) | copy-start | bytes 3538948
  101.6 6.0 %copy-start.9 = (bf16[3,1024,3,64]{1,3,2,0:T(8,128)(2,1)}, bf16[3,1024,3,64]{1,3,2,0:T(8,128)(2,1)S(1)}, u32[]{:S(2)}) copy-start(bf16[3,1024,3,64]{1,3,2,0:T(8,128)(2,1)S(1)} %get-tuple-element.395) | copy-start | bytes 3538948
  107.6 87.6 %copy-start.5 = (f32[3,1024,3,1,64]{1,4,3,2,0:T(8,128)S(1)}, f32[3,1024,3,1,64]{1,4,3,2,0:T(8,128)}, u32[]{:S(2)}) copy-start(f32[3,1024,3,1,64]{1,4,3,2,0:T(8,128)} %copy-done.4) | copy-start | bytes 7077892
  107.6 87.6 %copy-start.40 = (f32[3,64]{1,0:T(4,128)S(1)}, f32[3,64]{1,0:T(4,128)}, u32[]{:S(2)}) copy-start(f32[3,64]{1,0:T(4,128)} %param.20) | copy-start | bytes 2308
  123.3 6.0 %copy-start.1 = (bf16[3,1024,1024]{1,2,0:T(8,128)(2,1)S(1)}, bf16[3,1024,1024]{1,2,0:T(8,128)(2,1)}, u32[]{:S(2)}) copy-start(bf16[3,1024,1024]{1,2,0:T(8,128)(2,1)} %multiply_convert_fusion.6) | copy-start | bytes 18874372 | tf_op jit(solution)/shard_map/while
  152.4 6.0 %copy-start.1 = (bf16[3,1024,1024]{1,2,0:T(8,128)(2,1)S(1)}, bf16[3,1024,1024]{1,2,0:T(8,128)(2,1)}, u32[]{:S(2)}) copy-start(bf16[3,1024,1024]{1,2,0:T(8,128)(2,1)} %multiply_convert_fusion.6) | copy-start | bytes 18874372 | tf_op jit(solution)/shard_map/while
  181.5 6.0 %copy-start.1 = (bf16[3,1024,1024]{1,2,0:T(8,128)(2,1)S(1)}, bf16[3,1024,1024]{1,2,0:T(8,128)(2,1)}, u32[]{:S(2)}) copy-start(bf16[3,1024,1024]{1,2,0:T(8,128)(2,1)} %multiply_convert_fusion.6) | copy-start | bytes 18874372 | tf_op jit(solution)/shard_map/while
  195.2 2.6 copy-start.29
  195.2 2.6 copy-start.3
  195.2 3.1 copy-start.11
  195.2 3.1 copy-start.17
  195.2 3.1 copy-start.42
  198.3 1.7 copy-start.10
  198.3 1.7 copy-start.19
  198.3 1.7 copy-start.23
  198.4 1.7 copy-start.25
  203.6 3.1 slice-start
  204.4 2.3 slice-start.1
  207.1 29.4 %copy-start.14 = (bf16[3,1024,3,3,64]{1,4,3,2,0:T(8,128)(2,1)}, bf16[3,1024,3,3,64]{1,4,3,2,0:T(8,128)(2,1)S(1)}, u32[]{:S(2)}) copy-start(bf16[3,1024,3,3,64]{1,4,3,2,0:T(8,128)(2,1)S(1)} %copy.30) | copy-start | bytes 10616836
  236.5 35.4 %copy-start.13 = (bf16[3,1024,768]{2,1,0:T(8,128)(2,1)}, bf16[3,1024,768]{2,1,0:T(8,128)(2,1)S(1)}, u32[]{:S(2)}) copy-start(bf16[3,1024,768]{2,1,0:T(8,128)(2,1)S(1)} %get-tuple-element.159) | copy-start | bytes 14155780
  244.4 4.6 copy-start.44
  279.2 6.0 %copy-start.46 = (bf16[768,576]{0,1:T(8,128)(2,1)S(1)}, bf16[768,576]{0,1:T(8,128)(2,1)}, u32[]{:S(2)}) copy-start(bf16[768,576]{0,1:T(8,128)(2,1)} %param.19) | copy-start | bytes 2654212
  279.3 188.6 %reduce-scatter.5.cloned.1.call-start = ((), (), s32[]{:S(2)}) async-start(), calls=%async_computation.5 | async-start | bytes 5898240 | tf_op jit(solution)/shard_map/reduce_scatter | solution.py:134
  279.3 6.0 %copy-start.15 = (bf16[3,1024,3,3,64]{1,4,3,2,0:T(8,128)(2,1)S(1)}, bf16[3,1024,3,3,64]{1,4,3,2,0:T(8,128)(2,1)}, u32[]{:S(2)}) copy-start(bf16[3,1024,3,3,64]{1,4,3,2,0:T(8,128)(2,1)} %copy-done.14) | copy-start | bytes 10616836
  290.9 6.1 %copy-start.31 = (bf16[192,768]{1,0:T(8,128)(2,1)S(1)}, bf16[192,768]{1,0:T(8,128)(2,1)}, u32[]{:S(2)}) copy-start(bf16[192,768]{1,0:T(8,128)(2,1)} %param.22) | copy-start | bytes 884740
  291.0 227.1 %reduce-scatter.3.cloned.1.call-start = ((), (), s32[]{:S(2)}) async-start(), calls=%async_computation.3 | async-start | bytes 5898240 | tf_op jit(solution)/shard_map/reduce_scatter | solution.py:97
  418.5 2.9 copy-start.20
  421.5 1.6 copy-start.21
  421.5 2.9 copy-start.30
  423.0 44.8 %copy-start.7 = (bf16[3,256,768]{2,1,0:T(8,128)(2,1)S(1)}, bf16[3,256,768]{2,1,0:T(8,128)(2,1)}, u32[]{:S(2)}) copy-start(bf16[3,256,768]{2,1,0:T(8,128)(2,1)} %param.16) | copy-start | bytes 3538948
  423.0 44.8 %copy-start.33 = (f32[3,256]{1,0:T(4,128)S(1)}, f32[3,256]{1,0:T(4,128)}, u32[]{:S(2)}) copy-start(f32[3,256]{1,0:T(4,128)} %copy-done.32) | copy-start | bytes 9220
  423.1 44.8 %copy-start.35 = (f32[768]{0:T(1024)S(1)}, f32[768]{0:T(1024)}, u32[]{:S(2)}) copy-start(f32[768]{0:T(1024)} %param.18) | copy-start | bytes 9220
  423.1 47.5 %copy-start.37 = (f32[3,256]{1,0:T(4,128)S(1)}, f32[3,256]{1,0:T(4,128)}, u32[]{:S(2)}) copy-start(f32[3,256]{1,0:T(4,128)} %copy-done.36) | copy-start | bytes 9220
  467.8 2.7 copy-start.12
  (9 other events, 6.4 us)
Sparse Core Ops, SparseCore 0:
  13.5 40.1 all-gather.2
  55.2 37.4 all-gather.4
  279.4 139.1 all-reduce.4
  420.9 46.8 reduce-scatter.4
  470.2 47.8 reduce-scatter.2
where the time goes:
time: 580 us; the launch traced here: 569 us
  waiting for transfers between devices  216 us (37%)
  matrix products  169 us (29%)
  other arithmetic  91.3 us (16%)
  blocking collectives  62.1 us (11%)
  local copies, waits for them, and re-layouts  15.1 us (3%)
  between operations  14.8 us (3%)
    psum x1, waiting for transfers between devices, shards(): lax.psum(d_qkv.astype(jnp.bfloat16), 'dp').astype(jnp.float32)  92.2 us
    reduce_scatter x1, waiting for transfers between devices, shards(): lax.psum_scatter(partial_sum.astype(jnp.bfloat16), 'tp', scatter_dimensio...  45 us
    reduce_scatter x1, waiting for transfers between devices, shards(): lax.psum_scatter(d_normed.astype(jnp.bfloat16), 'tp', scatter_dimension=1...  42.6 us
    psum x1, blocking collectives, shards(): d_ln_gain, d_bias_two = lax.psum((d_ln_gain, d_bias_two), ('tp', 'dp'))  39.6 us
    all_gather x1, waiting for transfers between devices, shards(): normed = lax.all_gather(normed_local, 'tp', axis=1, tiled=True)  36 us
    convert_element_type x1, other arithmetic, shards(): active = gelu_exact(hidden).astype(jnp.bfloat16)  23 us
    psum x1, blocking collectives, shards(): lax.psum(d_q_gain.astype(jnp.bfloat16), 'dp').astype(jnp.float32)  22.5 us
    dot_general x3, matrix products, backward_keys(): jnp.einsum('hqk,qhd->khd', d_scores, queries, preferred_element_type=jnp....  17.9 us
  transfers between devices with their start and end apart: 5, of which 4 were waited for; matrix products, arithmetic and copies ran while one was open for 15% of the time, Pallas kernels for 0%

commit v1 on v0

--- a/solution.py
+++ b/solution.py
@@ -5,6 +5,22 @@
 
 epsilon = 1e-06
 masked_value = -1e30
+
+
+def gather_around(x, axis, dim):
+    ways, here, lap = (lax.axis_size(axis), lax.axis_index(axis), x.shape[dim])
+    shape = [n * ways if d == dim else n for d, n in enumerate(x.shape)]
+    full = lax.dynamic_update_slice_in_dim(jnp.zeros(shape, x.dtype), x, here * lap, axis=dim)
+    going_up = going_down = x
+    for far in range(1, ways // 2 + 1):
+        going_up = lax.ppermute(going_up, axis, [(d, (d + 1) % ways) for d in range(ways)])
+        full = lax.dynamic_update_slice_in_dim(full, going_up, (here - far) % ways * lap, axis=dim)
+        if 2 * far < ways:
+            going_down = lax.ppermute(going_down, axis, [(d, (d - 1) % ways) for d in range(ways)])
+            full = lax.dynamic_update_slice_in_dim(
+                full, going_down, (here + far) % ways * lap, axis=dim
+            )
+    return full
 
 
 def layer_norm(values, scale_gain):
@@ -73,7 +89,7 @@
     factor = head_size ** (-0.5)
     tokens_float = tokens.astype(jnp.float32)
     normed_local = layer_norm(tokens_float, ln_gain).astype(jnp.bfloat16)
-    normed = lax.all_gather(normed_local, "tp", axis=1, tiled=True)
+    normed = gather_around(normed_local, "tp", 1)
     seq_len = normed.shape[1]
     joined = jnp.einsum("bsd,dc->bsc", normed, w_qkv, preferred_element_type=jnp.float32)
     split_heads = joined.reshape(images, seq_len, heads_here, 3, head_size)

time: 580 us -> 598 us (1.031)
  local copies, waits for them, and re-layouts: 15.1 us -> 30.5 us
    all_gather x1 -> x0, waiting for transfers between devices: 36 us -> none  [shards(): normed = lax.all_gather(normed_local, 'tp', axis=1, tiled=True)]
    ppermute x0 -> x3, waiting for transfers between devices: none -> 25.7 us  [the longest x2 25.7 us: gather_around(): lax.ppermute(going_up, axis, [(d, (d + 1) % ways) for d in range(ways)])]
  transfers between devices with their start and end apart: 5 -> 7, of which waited for: 4 -> 5; matrix products, arithmetic and copies ran while one was open for 15% -> 22% of each run, Pallas kernels for 0% -> 0%
where the time goes in v1:
time: 598 us; the launch traced here: 591 us
  waiting for transfers between devices  211 us (35%)
  matrix products  171 us (29%)
  other arithmetic  89.8 us (15%)
  blocking collectives  67.8 us (11%)
  local copies, waits for them, and re-layouts  30.5 us (5%)
  between operations  15 us (3%)
    psum x1, waiting for transfers between devices, shards(): lax.psum(d_qkv.astype(jnp.bfloat16), 'dp').astype(jnp.float32)  98 us
    reduce_scatter x1, waiting for transfers between devices, shards(): lax.psum_scatter(partial_sum.astype(jnp.bfloat16), 'tp', scatter_dimensio...  45 us
    reduce_scatter x1, waiting for transfers between devices, shards(): lax.psum_scatter(d_normed.astype(jnp.bfloat16), 'tp', scatter_dimension=1...  42.7 us
    psum x1, blocking collectives, shards(): d_ln_gain, d_bias_two = lax.psum((d_ln_gain, d_bias_two), ('tp', 'dp'))  39.6 us
    psum x1, blocking collectives, shards(): lax.psum(d_q_gain.astype(jnp.bfloat16), 'dp').astype(jnp.float32)  28.2 us
    ppermute x2, waiting for transfers between devices, gather_around(): lax.ppermute(going_up, axis, [(d, (d + 1) % ways) for d in range(ways)])  25.7 us
    convert_element_type x1, other arithmetic, shards(): active = gelu_exact(hidden).astype(jnp.bfloat16)  23 us
    dot_general x3, matrix products, backward_keys(): jnp.einsum('hqk,qhd->khd', d_scores, queries, preferred_element_type=jnp....  17.9 us
  transfers between devices with their start and end apart: 7, of which 5 were waited for; matrix products, arithmetic and copies ran while one was open for 22% of the time, Pallas kernels for 0%

profile of v1, /device:TPU:0, one launch (start us, length us, event | category | flops | bytes accessed | tf_op | source)
XLA Modules:
  0.0 591.1 jit_solution(9031071793622279805)
XLA Ops:
  14.3 24.0 %collective-permute-done = bf16[3,256,768]{2,1,0:T(8,128)(2,1)} collective-permute-done((bf16[3,256,768]{2,1,0:T(8,128)(2,1)S(1)}, bf16[3,256,768]{2,1,0:T(8,128)(2,1)}, u32[]{:S(2)}, u32[]{:S(2)}) %collective-permute-start) | collective-permute-done | bytes 1179680 | tf_op jit(solution)/shard_map/ppermute | solution.py:16
  58.8 4.8 fusion.86
  69.3 37.3 %while.28 = (s32[]{:T(128)}, bf16[3,1024,3,64]{1,3,2,0:T(8,128)(2,1)}, f32[3,3,1024]{2,1,0:T(4,128)}, bf16[3,1024,3,64]{1,3,2,0:T(8,128)(2,1)}, s32[3]{0:T(128)S...) while((s32[]{:T(128)}, bf16[3,1024,3,64]{1,3,2,0:T(8,128)(2,1)}, ...), condition=%wide.region_9.10_spmd.clone, body=%wide.region_6.9_spmd.sunk.clone | while | flops 843053056 | bytes 39823964 | solution.py:105
  73.1 3.2 fusion.152
  76.9 4.9 fusion.153
  85.5 3.2 fusion.152
  89.3 4.9 fusion.153
  97.8 3.2 fusion.152
  101.6 4.9 fusion.153
  106.6 9.3 %fusion.72 = (u8[1024,768]{1,0:T(8,128)(4,1)S(1)}, u8[1024,768]{1,0:T(8,128)(4,1)S(1)}, f32[3,1024,768]{2,1,0:T(8,128)S(1)}) fusion(f32[768]{0:T(1024)S(1)} %copy-done.44, bf16[3,1024,768]{1,2,0:T(8,128)(2,1)} %constant_dynamic-update-slice_fusion, bf16[768,768]{1,0:T(8,128)(2,1)S(1)} %copy-done), kind=kOutput, calls=%fused_computation.122 | convolution fusion | flops 3655335936 | bytes 16911360 | tf_op jit(solution)/shard_map/bsd,df->bsf/dot_general | solution.py:107
  115.9 3.7 copy-done.13
  119.6 23.0 %multiply_convert_fusion.1 = (bf16[3,1024,768]{2,1,0:T(8,128)(2,1)}, f32[3,1024,768]{2,1,0:T(8,128)}) fusion(f32[3,1024,768]{2,1,0:T(8,128)S(1)} %get-tuple-element.172, f32[768]{0:T(1024)S(1)} %copy-done.44, u8[1024,768]{1,0:T(8,128)(4,1)S(1)} %get-tuple-element.109, u8[1024,768]{1,0:T(8,128)(4,1)S(1)} %get-tuple-element.108), kind=kLoop, calls=%fused_computation.70 | loop fusion | flops 167510016 | bytes 25168896 | tf_op jit(solution)/shard_map/convert_element_type | solution.py:108
  142.6 5.0 convolution_convert_fusion
  147.6 88.0 %while.29 = (s32[]{:T(128)}, f32[3,1024,3,64]{1,3,2,0:T(8,128)}, f32[3,1024,3,64]{1,3,2,0:T(8,128)}, bf16[3,1024,3,64]{1,3,2,0:T(8,128)(2,1)}, bf16[3,1024,3,64]...) while((s32[]{:T(128)}, f32[3,1024,3,64]{1,3,2,0:T(8,128)}, ...), condition=%wide.region_13.14_spmd.clone, body=%wide.region_11.13_spmd.sunk.clone | while | flops 2060843008 | bytes 124744848 | solution.py:134
  148.0 3.1 fusion.162
  153.1 4.8 multiply_reduce_fusion.9
  157.9 5.7 multiply_convert_fusion.6
  163.6 6.0 %fusion.164 = f32[3,1024,3,64]{1,3,2,0:T(8,128)} fusion(f32[3,1024,3,64]{1,3,2,0:T(8,128)} %get-tuple-element.364, s32[]{:T(128)} %get-tuple-element.362, bf16[3,1024,1024]{1,2,0:T(8,128)(2,1)} %multiply_convert_fusion.6, bf16[3,1024,3,64]{1,3,2,0:T(8,128)(2,1)} %get-tuple-element.378), kind=kOutput, calls=%fused_computation.31.clone.1.clone | convolution fusion | flops 402849792 | bytes 7472128 | tf_op jit(solution)/shard_map/while/body/eval_jaxpr/hqk,qhd->khd/dot_general | solution.py:72
  169.6 3.1 fusion.163
  172.7 4.6 fusion.165
  177.3 2.9 fusion.162
  182.2 4.8 multiply_reduce_fusion.9
  187.1 5.7 multiply_convert_fusion.6
  192.8 6.0 %fusion.164 = f32[3,1024,3,64]{1,3,2,0:T(8,128)} fusion(f32[3,1024,3,64]{1,3,2,0:T(8,128)} %get-tuple-element.364, s32[]{:T(128)} %get-tuple-element.362, bf16[3,1024,1024]{1,2,0:T(8,128)(2,1)} %multiply_convert_fusion.6, bf16[3,1024,3,64]{1,3,2,0:T(8,128)(2,1)} %get-tuple-element.378), kind=kOutput, calls=%fused_computation.31.clone.1.clone | convolution fusion | flops 402849792 | bytes 7472128 | tf_op jit(solution)/shard_map/while/body/eval_jaxpr/hqk,qhd->khd/dot_general | solution.py:72
  198.7 3.1 fusion.163
  201.8 4.6 fusion.165
  206.5 2.9 fusion.162
  211.4 4.8 multiply_reduce_fusion.9
  216.2 5.7 multiply_convert_fusion.6
  221.9 6.0 %fusion.164 = f32[3,1024,3,64]{1,3,2,0:T(8,128)} fusion(f32[3,1024,3,64]{1,3,2,0:T(8,128)} %get-tuple-element.364, s32[]{:T(128)} %get-tuple-element.362, bf16[3,1024,1024]{1,2,0:T(8,128)(2,1)} %multiply_convert_fusion.6, bf16[3,1024,3,64]{1,3,2,0:T(8,128)(2,1)} %get-tuple-element.378), kind=kOutput, calls=%fused_computation.31.clone.1.clone | convolution fusion | flops 402849792 | bytes 7472128 | tf_op jit(solution)/shard_map/while/body/eval_jaxpr/hqk,qhd->khd/dot_general | solution.py:72
  227.9 3.1 fusion.163
  231.0 4.6 fusion.165
  246.8 7.8 %bitcast_convert_fusion.2 = bf16[768,576]{0,1:T(8,128)(2,1)} fusion(bf16[3,1024,768]{1,2,0:T(8,128)(2,1)} %constant_dynamic-update-slice_fusion, bf16[3,1024,576]{1,2,0:T(8,128)(2,1)S(1)} %bitcast.228), kind=kOutput, calls=%fused_computation.125 | convolution fusion | flops 2718351360 | bytes 9142272 | tf_op jit(solution)/shard_map/bsd,bsc->dc/dot_general | solution.py:146
  254.7 14.3 %fusion.98 = (bf16[768]{0:T(1024)(128)(2,1)S(1)}, bf16[3,1024,768]{2,1,0:T(8,128)(2,1)}) fusion(f32[3,1024,768]{2,1,0:T(8,128)} %get-tuple-element.160, bf16[3,1024,768]{2,1,0:T(8,128)(2,1)} %all-gather.2.cloned.1.call-done, bf16[768,768]{1,0:T(8,128)(2,1)S(1)} %copy-done.46, f32[3,1024,768]{2,1,0:T(8,128)S(1)} %bitcast.223, f32[768]{0:T(1024)S(1)} %copy-done.45), kind=kOutput, calls=%fused_computation.169 | convolution fusion | flops 3661626624 | bytes 29495808 | tf_op jit(solution)/shard_map/bsd,fd->bsf/dot_general | solution.py:120
  269.0 8.6 %bitcast_convert_fusion.1 = bf16[768,768]{1,0:T(8,128)(2,1)} fusion(bf16[3,1024,768]{1,2,0:T(8,128)(2,1)} %constant_dynamic-update-slice_fusion, bf16[3,1024,768]{2,1,0:T(8,128)(2,1)} %get-tuple-element.174), kind=kOutput, calls=%fused_computation.108 | convolution fusion | flops 3624468480 | bytes 10616832 | tf_op jit(solution)/shard_map/bsd,bsf->df/dot_general | solution.py:123
  277.6 4.5 fusion.74
  282.1 7.3 %bitcast_convert_fusion = bf16[768,768]{1,0:T(8,128)(2,1)} fusion(bf16[3,1024,768]{2,1,0:T(8,128)(2,1)S(1)} %bitcast.227, bf16[3,1024,768]{2,1,0:T(8,128)(2,1)} %all-gather.2.cloned.1.call-done), kind=kOutput, calls=%fused_computation.107 | convolution fusion | flops 3624468480 | bytes 10616832 | tf_op jit(solution)/shard_map/bsf,bsd->fd/dot_general | solution.py:118
  289.6 5.9 %fusion.81 = f32[3,1024,768]{2,1,0:T(8,128)S(1)} fusion(bf16[3,1024,768]{2,1,0:T(8,128)(2,1)} %get-tuple-element.174, bf16[768,768]{1,0:T(8,128)(2,1)S(1)} %copy-done), kind=kOutput, calls=%fused_computation.136 | convolution fusion | flops 3623878656 | bytes 15335424 | tf_op jit(solution)/shard_map/bsf,df->bsd/dot_general | solution.py:125
  295.5 5.6 add_convert_fusion
  301.3 6.1 %fusion.79 = f32[3,1024,768]{2,1,0:T(8,128)S(1)} fusion(bf16[3,1024,768]{2,1,0:T(8,128)(2,1)} %get-tuple-element.159, bf16[768,768]{1,0:T(8,128)(2,1)S(1)} %copy-done.46), kind=kOutput, calls=%fused_computation.134 | convolution fusion | flops 3623878656 | bytes 15335424 | tf_op jit(solution)/shard_map/bsf,fd->bsd/dot_general | solution.py:110
  307.3 5.0 add_convert_fusion.2
  312.3 28.2 %all-reduce.1 = (bf16[3,64]{1,0:T(4,128)(2,1)S(1)}, bf16[3,64]{1,0:T(4,128)(2,1)S(1)}, bf16[768]{0:T(1024)(128)(2,1)S(1)}) all-reduce(bf16[3,64]{1,0:T(4,128)(2,1)S(1)} %get-tuple-element.176, bf16[3,64]{1,0:T(4,128)(2,1)S(1)} %get-tuple-element.110, bf16[768]{0:T(1024)(128)(2,1)S(1)} %get-tuple-element.173), channel_id=1, replica_groups=mesh['tp'=4,'dp'=8] {'dp'}, use_global_device_ids=true, to_apply=%region_25.26 | all-reduce | flops 1152 | bytes 4608 | tf_op jit(solution)/shard_map/psum | solution.py:160
  342.3 98.0 %all-reduce.5.cloned.1.call-done = (bf16[768,576]{0,1:T(8,128)(2,1)}, bf16[192,768]{1,0:T(8,128)(2,1)}, bf16[768,768]{1,0:T(8,128)(2,1)}, bf16[768,768]{1,0:T(8,128)(2,1)}) async-done(((bf16[768,576]{0,1:T(8,128)(2,1)}, bf16[192,768]{1,0:T(8,128)(2,1)}, bf16[768,768]{1,0:T(8,128)(2,1)}, bf16[768,768]{1,0:T(8,128)(2,1)}), (bf16[768,576]{0,1:T(8,128)(2,1)}, bf16[192,768]{1,0:T(8,128)(2,1)}, ...) | async-done | bytes 3538960 | tf_op jit(solution)/shard_map/psum | solution.py:159
  440.3 2.9 convert_element_type.130
  447.0 42.7 %reduce-scatter.5.cloned.1.call-done = bf16[3,256,768]{2,1,0:T(8,128)(2,1)} async-done(((bf16[3,1024,768]{2,1,0:T(8,128)(2,1)}), bf16[3,256,768]{2,1,0:T(8,128)(2,1)}) %reduce-scatter.5.cloned.1.call-update) | async-done | bytes 1179664 | tf_op jit(solution)/shard_map/reduce_scatter | solution.py:150
  495.0 45.0 %reduce-scatter.3.cloned.1.call-done = bf16[3,256,768]{2,1,0:T(8,128)(2,1)} async-done(((bf16[3,1024,768]{2,1,0:T(8,128)(2,1)}), bf16[3,256,768]{2,1,0:T(8,128)(2,1)}) %reduce-scatter.3.cloned.1.call-update) | async-done | bytes 1179664 | tf_op jit(solution)/shard_map/reduce_scatter | solution.py:113
  540.0 4.5 convert_reduce_fusion.1
  544.5 39.6 %all-reduce = (f32[768]{0:T(1024)}, f32[768]{0:T(1024)}) all-reduce(f32[768]{0:T(1024)} %get-tuple-element.114, f32[768]{0:T(1024)} %get-tuple-element.169), channel_id=1, replica_groups=mesh['tp'=4,'dp'=8] {'tp','dp'}, use_global_device_ids=true, to_apply=%region_22.23 | all-reduce | flops 1536 | bytes 12288 | tf_op jit(solution)/shard_map/psum | solution.py:157
  (202 shorter events, 73.5 us)
Async XLA Ops:
  7.2 99.4 %copy-start = (bf16[768,768]{1,0:T(8,128)(2,1)S(1)}, bf16[768,768]{1,0:T(8,128)(2,1)}, u32[]{:S(2)}) copy-start(bf16[768,768]{1,0:T(8,128)(2,1)} %param.23) | copy-start | bytes 3538948
  7.2 4.1 copy-start.6
  7.2 4.1 copy-start.35
  7.2 135.4 %all-gather.2.cloned.1.call-start = ((), (), s32[]{:S(2)}) async-start(), calls=%async_computation.3 | async-start | bytes 5898240 | tf_op jit(solution)/shard_map/all_gather | solution.py:117
  8.9 29.3 %copy-start.33 = (f32[3,256]{1,0:T(4,128)}, f32[3,256]{1,0:T(4,128)S(1)}, u32[]{:S(2)}) copy-start(f32[3,256]{1,0:T(4,128)S(1)} %broadcast_multiply_fusion.2) | copy-start | bytes 9220
  11.3 27.0 %copy-start.37 = (f32[3,256]{1,0:T(4,128)}, f32[3,256]{1,0:T(4,128)S(1)}, u32[]{:S(2)}) copy-start(f32[3,256]{1,0:T(4,128)S(1)} %fusion.94) | copy-start | bytes 9220
  11.7 26.5 %collective-permute-start = (bf16[3,256,768]{2,1,0:T(8,128)(2,1)S(1)}, bf16[3,256,768]{2,1,0:T(8,128)(2,1)}, u32[]{:S(2)}, u32[]{:S(2)}) collective-permute-start(bf16[3,256,768]{2,1,0:T(8,128)(2,1)S(1)} %fusion.65), channel_id=1, source_target_pairs={{0,8},{8,16},{16,24},{24,0},{1,9},{9,17},{17,25},{25,1},{2,10},{10... | collective-permute-start | bytes 3538952 | tf_op jit(solution)/shard_map/ppermute | solution.py:16
  12.3 38.2 %collective-permute-start.1 = (bf16[3,256,768]{2,1,0:T(8,128)(2,1)S(1)}, bf16[3,256,768]{2,1,0:T(8,128)(2,1)}, u32[]{:S(2)}, u32[]{:S(2)}) collective-permute-start(bf16[3,256,768]{2,1,0:T(8,128)(2,1)S(1)} %fusion.65), channel_id=1, source_target_pairs={{0,24},{8,0},{16,8},{24,16},{1,25},{9,1},{17,9},{25,17},{2,26},{10... | collective-permute-start | bytes 3538952 | tf_op jit(solution)/shard_map/ppermute | solution.py:19
  38.2 17.8 %collective-permute-start.2 = (bf16[3,256,768]{2,1,0:T(8,128)(2,1)}, bf16[3,256,768]{2,1,0:T(8,128)(2,1)}, u32[]{:S(2)}, u32[]{:S(2)}) collective-permute-start(bf16[3,256,768]{2,1,0:T(8,128)(2,1)} %collective-permute-done), channel_id=1, source_target_pairs={{0,8},{8,16},{16,24},{24,0},{1,9},{9,17},{17,25},{25,1},{2,10},{10... | collective-permute-start | bytes 3538952 | tf_op jit(solution)/shard_map/ppermute | solution.py:16
  40.6 399.7 %all-reduce.5.cloned.1.call-start = ((), (), s32[]{:S(2)}) async-start(), calls=%async_computation.5 | async-start | bytes 7077888 | tf_op jit(solution)/shard_map/psum | solution.py:159
  54.3 4.4 copy-start.47
  64.3 3.7 copy-start.4
  64.3 4.2 copy-start.2
  69.3 37.3 %copy-start.44 = (f32[768]{0:T(1024)S(1)}, f32[768]{0:T(1024)}, u32[]{:S(2)}) copy-start(f32[768]{0:T(1024)} %param.24) | copy-start | bytes 9220
  106.6 9.4 %copy-start.8 = (bf16[3,1024,3,64]{1,3,2,0:T(8,128)(2,1)}, bf16[3,1024,3,64]{1,3,2,0:T(8,128)(2,1)S(1)}, u32[]{:S(2)}) copy-start(bf16[3,1024,3,64]{1,3,2,0:T(8,128)(2,1)S(1)} %get-tuple-element.393) | copy-start | bytes 3538948
  106.6 9.4 %copy-start.9 = (bf16[3,1024,3,64]{1,3,2,0:T(8,128)(2,1)}, bf16[3,1024,3,64]{1,3,2,0:T(8,128)(2,1)S(1)}, u32[]{:S(2)}) copy-start(bf16[3,1024,3,64]{1,3,2,0:T(8,128)(2,1)S(1)} %get-tuple-element.394) | copy-start | bytes 3538948
  115.9 3.7 copy-start.13
  119.6 23.0 %copy-start.31 = (bf16[192,768]{1,0:T(8,128)(2,1)S(1)}, bf16[192,768]{1,0:T(8,128)(2,1)}, u32[]{:S(2)}) copy-start(bf16[192,768]{1,0:T(8,128)(2,1)} %param.22) | copy-start | bytes 884740
  147.6 88.0 %copy-start.5 = (f32[3,1024,3,1,64]{1,4,3,2,0:T(8,128)S(1)}, f32[3,1024,3,1,64]{1,4,3,2,0:T(8,128)}, u32[]{:S(2)}) copy-start(f32[3,1024,3,1,64]{1,4,3,2,0:T(8,128)} %copy-done.4) | copy-start | bytes 7077892
  147.6 88.0 %copy-start.41 = (f32[3,64]{1,0:T(4,128)S(1)}, f32[3,64]{1,0:T(4,128)}, u32[]{:S(2)}) copy-start(f32[3,64]{1,0:T(4,128)} %param.20) | copy-start | bytes 2308
  163.6 6.0 %copy-start.1 = (bf16[3,1024,1024]{1,2,0:T(8,128)(2,1)S(1)}, bf16[3,1024,1024]{1,2,0:T(8,128)(2,1)}, u32[]{:S(2)}) copy-start(bf16[3,1024,1024]{1,2,0:T(8,128)(2,1)} %multiply_convert_fusion.6) | copy-start | bytes 18874372 | tf_op jit(solution)/shard_map/while
  192.8 6.0 %copy-start.1 = (bf16[3,1024,1024]{1,2,0:T(8,128)(2,1)S(1)}, bf16[3,1024,1024]{1,2,0:T(8,128)(2,1)}, u32[]{:S(2)}) copy-start(bf16[3,1024,1024]{1,2,0:T(8,128)(2,1)} %multiply_convert_fusion.6) | copy-start | bytes 18874372 | tf_op jit(solution)/shard_map/while
  221.9 6.0 %copy-start.1 = (bf16[3,1024,1024]{1,2,0:T(8,128)(2,1)S(1)}, bf16[3,1024,1024]{1,2,0:T(8,128)(2,1)}, u32[]{:S(2)}) copy-start(bf16[3,1024,1024]{1,2,0:T(8,128)(2,1)} %multiply_convert_fusion.6) | copy-start | bytes 18874372 | tf_op jit(solution)/shard_map/while
  235.6 2.6 copy-start.27
  235.6 2.6 copy-start.3
  235.6 3.1 copy-start.11
  235.7 3.1 copy-start.17
  235.7 3.1 copy-start.43
  246.1 8.5 %slice-start = ((s8[9437184]{0:T(1024)(128)(4,1)}), s8[4194304]{0:T(1024)(128)(4,1)S(1)}, s32[]{:S(2)}) async-start(s8[9437184]{0:T(1024)(128)(4,1)} %bitcast.222), calls=%async_computation.6 | async-start | bytes 8388608
  246.7 7.9 %copy-start.14 = (bf16[3,1024,3,3,64]{1,4,3,2,0:T(8,128)(2,1)}, bf16[3,1024,3,3,64]{1,4,3,2,0:T(8,128)(2,1)S(1)}, u32[]{:S(2)}) copy-start(bf16[3,1024,3,3,64]{1,4,3,2,0:T(8,128)(2,1)S(1)} %copy.36) | copy-start | bytes 10616836
  246.7 7.9 %slice-start.1 = ((s8[9437184]{0:T(1024)(128)(4,1)}), s8[4194304]{0:T(1024)(128)(4,1)S(1)}, s32[]{:S(2)}) async-start(s8[9437184]{0:T(1024)(128)(4,1)} %bitcast.222), calls=%async_computation.7 | async-start | bytes 8388608
  246.8 7.9 %slice-start.2 = ((s8[9437184]{0:T(1024)(128)(4,1)}), s8[1048576]{0:T(1024)(128)(4,1)S(1)}, s32[]{:S(2)}) async-start(s8[9437184]{0:T(1024)(128)(4,1)} %bitcast.222), calls=%async_computation.8 | async-start | bytes 2097152
  246.8 7.9 %copy-start.45 = (f32[768]{0:T(1024)S(1)}, f32[768]{0:T(1024)}, u32[]{:S(2)}) copy-start(f32[768]{0:T(1024)} %param.24) | copy-start | bytes 9220
  246.8 7.9 %copy-start.46 = (bf16[768,768]{1,0:T(8,128)(2,1)S(1)}, bf16[768,768]{1,0:T(8,128)(2,1)}, u32[]{:S(2)}) copy-start(bf16[768,768]{1,0:T(8,128)(2,1)} %param.25) | copy-start | bytes 3538948
  246.8 35.4 %slice-start.3 = ((s8[4718592]{0:T(1024)(128)(4,1)}), s8[4194304]{0:T(1024)(128)(4,1)S(1)}, s32[]{:S(2)}) async-start(s8[4718592]{0:T(1024)(128)(4,1)} %bitcast.226), calls=%async_computation.9 | async-start | bytes 8388608
  254.7 27.5 %slice-start.4 = ((s8[4718592]{0:T(1024)(128)(4,1)}), s8[524288]{0:T(1024)(128)(4,1)S(1)}, s32[]{:S(2)}) async-start(s8[4718592]{0:T(1024)(128)(4,1)} %bitcast.226), calls=%async_computation.10 | async-start | bytes 1048576
  289.5 6.0 %copy-start.48 = (bf16[768,576]{0,1:T(8,128)(2,1)S(1)}, bf16[768,576]{0,1:T(8,128)(2,1)}, u32[]{:S(2)}) copy-start(bf16[768,576]{0,1:T(8,128)(2,1)} %param.19) | copy-start | bytes 2654212
  289.5 200.3 %reduce-scatter.5.cloned.1.call-start = ((), (), s32[]{:S(2)}) async-start(), calls=%async_computation.4 | async-start | bytes 5898240 | tf_op jit(solution)/shard_map/reduce_scatter | solution.py:150
  289.6 6.0 %copy-start.15 = (bf16[3,1024,3,3,64]{1,4,3,2,0:T(8,128)(2,1)S(1)}, bf16[3,1024,3,3,64]{1,4,3,2,0:T(8,128)(2,1)}, u32[]{:S(2)}) copy-start(bf16[3,1024,3,3,64]{1,4,3,2,0:T(8,128)(2,1)} %copy-done.14) | copy-start | bytes 10616836
  301.2 6.1 %copy-start.32 = (bf16[192,768]{1,0:T(8,128)(2,1)S(1)}, bf16[192,768]{1,0:T(8,128)(2,1)}, u32[]{:S(2)}) copy-start(bf16[192,768]{1,0:T(8,128)(2,1)} %param.22) | copy-start | bytes 884740
  301.2 238.8 %reduce-scatter.3.cloned.1.call-start = ((), (), s32[]{:S(2)}) async-start(), calls=%async_computation.2 | async-start | bytes 5898240 | tf_op jit(solution)/shard_map/reduce_scatter | solution.py:113
  440.3 2.9 copy-start.20
  443.2 2.9 copy-start.30
  444.8 45.0 %copy-start.7 = (bf16[3,256,768]{2,1,0:T(8,128)(2,1)S(1)}, bf16[3,256,768]{2,1,0:T(8,128)(2,1)}, u32[]{:S(2)}) copy-start(bf16[3,256,768]{2,1,0:T(8,128)(2,1)} %param.16) | copy-start | bytes 3538948
  444.8 45.0 %copy-start.34 = (f32[3,256]{1,0:T(4,128)S(1)}, f32[3,256]{1,0:T(4,128)}, u32[]{:S(2)}) copy-start(f32[3,256]{1,0:T(4,128)} %copy-done.33) | copy-start | bytes 9220
  444.8 45.0 %copy-start.36 = (f32[768]{0:T(1024)S(1)}, f32[768]{0:T(1024)}, u32[]{:S(2)}) copy-start(f32[768]{0:T(1024)} %param.18) | copy-start | bytes 9220
  444.8 47.7 %copy-start.38 = (f32[3,256]{1,0:T(4,128)S(1)}, f32[3,256]{1,0:T(4,128)}, u32[]{:S(2)}) copy-start(f32[3,256]{1,0:T(4,128)} %copy-done.37) | copy-start | bytes 9220
  489.8 2.7 copy-start.12
  (16 other events, 20.1 us)
Sparse Core Ops, SparseCore 0:
  40.7 41.0 all-gather.1
  289.6 150.6 all-reduce.4
  442.8 46.8 reduce-scatter.4
  492.2 47.8 reduce-scatter.2
